TPU v7x, 512 devices: a whole 4x8x8 slice. The times are simulated.
512 devices in a mesh: dp: 64 (over y, z), fsdp: 8 (over x, core).
Axes of the slice: x: 4, y: 8, z: 8, core: 2. Of those that a mesh axis runs over, the one named last changes fastest.
Arguments:
- frames: bfloat16 [524288, 512], P(('dp', 'fsdp')), may hold values from -6 to 6
- utt_pairs: int32 [8, 64, 4], P('fsdp'), may hold values from 32 to 256, as said below
- utt_dest: int32 [8, 64, 4], P('fsdp'), may hold values from 0 to 63, as said below
- conv_weight: bfloat16 [1536, 512], P('dp'), may hold values from -0.15625 to 0.15625
- proj_weight: bfloat16 [512, 1536], P('dp'), may hold values from -0.25 to 0.25
- point_weight: bfloat16 [2, 1536, 1536], P(None, None, 'fsdp'), may hold values from -0.15625 to 0.15625
- depth_weight: float32 [31, 1536], replicated, may hold values from -1 to 1
- gain_first: float32 [1536], replicated, may hold values from 0.5 to 1.5
- gain_second: float32 [1536], replicated, may hold values from 0.5 to 1.5
Outputs:
- encoded: bfloat16 [262144, 1536], P(('dp', 'fsdp'))
Inputs may be any that keep to these rules, and one draw needn't show every extreme that they name: `utt_pairs`: every loader holds exactly 512 pairs and every sequence device receives exactly 512 pairs, from 4 different loaders. Each loader holds one utterance of exactly 256 pairs and one of exactly 32 pairs. `utt_dest`: the 4 utterances of loader i go to the 4 different sequence devices (i + k * 64 / 4) mod 64, k = 0 .. 3, in some order.
All inputs are finite; a program needn't handle non-finite values.
Results may differ from a plain program's by a relative error of at most 0.012.
Values may be sent and summed in bfloat16 or wider, within the bound.
No kernel may reach another device: no remote copies, remote signals or barrier semaphores. Data moves between devices by JAX's collectives and lax.ppermute only.
A program may use at most 64 MiB of HBM per device.

v0:
```python
import jax
import jax.numpy as jnp
from jax import lax
from jax.sharding import PartitionSpec as P


def passed_along(value, axis, steps):
    count = lax.axis_size(axis)
    pairs = [(source, (source + steps) % count) for source in range(count)]
    return lax.ppermute(value, axis, pairs)


def frontend(pair_rows, first_rows, conv_full):
    channels = pair_rows.shape[1] // 2
    even_frames = pair_rows[:, :channels]
    odd_frames = pair_rows[:, channels:]
    earlier = jnp.pad(odd_frames[:-1], ((1, 0), (0, 0)))
    earlier = jnp.where(first_rows[:, None], jnp.zeros_like(earlier), earlier)
    summed = jnp.dot(earlier, conv_full[:channels], preferred_element_type=jnp.float32)
    summed = summed + jnp.dot(
        even_frames, conv_full[channels : 2 * channels], preferred_element_type=jnp.float32
    )
    summed = summed + jnp.dot(
        odd_frames, conv_full[2 * channels :], preferred_element_type=jnp.float32
    )
    return jax.nn.relu(summed).astype(jnp.bfloat16)


def layer_norm(values, scales):
    centered = values - jnp.mean(values, axis=-1, keepdims=True)
    variance = jnp.mean(centered * centered, axis=-1, keepdims=True)
    return centered * lax.rsqrt(variance + 1e-05) * scales


def depthwise(gated, depth_weight, positions, lengths):
    row_count = gated.shape[0]
    kernel_size = depth_weight.shape[0]
    half_width = kernel_size // 2
    padded = jnp.pad(gated.astype(jnp.float32), ((half_width, half_width), (0, 0)))
    mixed = jnp.zeros(gated.shape, jnp.float32)
    for tap_index in range(kernel_size):
        offset = tap_index - half_width
        inside = (positions + offset >= 0) & (positions + offset < lengths)
        term = padded[tap_index : tap_index + row_count] * depth_weight[tap_index][None, :]
        mixed = mixed + jnp.where(inside[:, None], term, jnp.zeros_like(term))
    return mixed


def gate_product(normed, value_weight, gate_weight):
    value_part = jnp.dot(normed, value_weight, preferred_element_type=jnp.float32)
    gate_part = jnp.dot(normed, gate_weight, preferred_element_type=jnp.float32)
    return (value_part * jax.nn.sigmoid(gate_part)).astype(jnp.bfloat16)


def cut_pieces(source_rows, own_starts, slot_size, utt_count):
    padded = jnp.pad(source_rows, ((0, slot_size), (0, 0)))
    pieces = []
    for slot_index in range(utt_count):
        pieces.append(lax.dynamic_slice_in_dim(padded, own_starts[slot_index], slot_size, 0))
    return pieces


def body(
    frames,
    utt_pairs,
    utt_dest,
    conv_weight,
    proj_weight,
    point_weight,
    depth_weight,
    gain_first,
    gain_second,
):
    node_count = lax.axis_size("dp")
    own_index = lax.axis_index("dp")
    pair_count = frames.shape[0] // 2
    channels = frames.shape[1]
    utt_count = utt_pairs.shape[2]
    spacing = node_count // utt_count
    slot_size = pair_count // 2
    pair_table = utt_pairs[0]
    dest_table = utt_dest[0]
    loader_ids = jnp.arange(node_count, dtype=jnp.int32)
    slot_ids = jnp.arange(utt_count, dtype=jnp.int32)
    slot_table = (dest_table - loader_ids[:, None]) % node_count // spacing
    matches = (slot_table[:, :, None] == slot_ids[None, None, :]).astype(jnp.int32)
    loader_offsets = jnp.cumsum(pair_table, axis=1) - pair_table
    slot_counts = jnp.sum(matches * pair_table[:, :, None], axis=1)
    slot_starts = jnp.sum(matches * loader_offsets[:, :, None], axis=1)
    conv_full, proj_full = (
        lax.all_gather(conv_weight, "dp", axis=0, tiled=True),
        lax.all_gather(proj_weight, "dp", axis=0, tiled=True),
    )
    own_starts = slot_starts[own_index]
    sources = (own_index - slot_ids * spacing) % node_count
    piece_lengths = slot_counts[sources, slot_ids]
    earlier_pieces = (sources[None, :] < sources[:, None]).astype(jnp.int32)
    piece_offsets = jnp.sum(earlier_pieces * piece_lengths[None, :], axis=1)
    pair_rows = jnp.arange(pair_count, dtype=jnp.int32)
    inside = (
        (pair_rows[:, None] >= piece_offsets[None, :])
        & (pair_rows[:, None] < piece_offsets[None, :] + piece_lengths[None, :])
    ).astype(jnp.int32)
    piece_index = jnp.sum(inside * slot_ids[None, :], axis=1)
    positions = pair_rows - jnp.sum(inside * piece_offsets[None, :], axis=1)
    lengths = jnp.sum(inside * piece_lengths[None, :], axis=1)
    flat_slot = piece_index * slot_size + positions
    frame_pairs = frames.reshape(pair_count, 2 * channels)
    pieces = cut_pieces(frame_pairs, own_starts, slot_size, utt_count)
    arrived = [pieces[0]]
    for slot_index in range(1, utt_count):
        arrived.append(passed_along(pieces[slot_index], "dp", slot_index * spacing))
    stacked = jnp.concatenate(arrived, axis=0)
    packed = jnp.take(stacked, flat_slot, axis=0)
    front = frontend(packed, positions == 0, conv_full)
    projected = jnp.dot(front, proj_full, preferred_element_type=jnp.float32).astype(jnp.bfloat16)
    normed = layer_norm(projected.astype(jnp.float32), gain_first).astype(jnp.bfloat16)
    weight_part = lax.all_gather(point_weight, "fsdp", axis=2, tiled=True)
    gated = gate_product(normed, weight_part[0], weight_part[1])
    mixed = depthwise(gated, depth_weight, positions, lengths)
    scaled = layer_norm(mixed, gain_second)
    return (scaled * jax.nn.sigmoid(scaled)).astype(jnp.bfloat16)


def solution(mesh):
    in_specs = (
        P(("dp", "fsdp"), None),
        P("fsdp", None, None),
        P("fsdp", None, None),
        P("dp", None),
        P("dp", None),
        P(None, None, "fsdp"),
        P(),
        P(),
        P(),
    )
    out_specs = P(("dp", "fsdp"), None)
    return jax.shard_map(body, mesh=mesh, in_specs=in_specs, out_specs=out_specs, check_vma=False)
```

profile of v0, /device:TPU:1, one launch (start us, length us, event | category | flops | bytes accessed | tf_op | source)
XLA Modules:
  0.0 303.4 jit_solution(6321874885541037050)
XLA Ops:
  6.5 0.7 all-gather.4.cloned.1.call-update
  8.8 0.8 reduce_window_sum.11
  9.5 0.7 add_select_fusion
  16.7 1.4 reshape.518
  20.7 1.6 pad_dynamic-slice_fusion.3
  22.2 5.1 %collective-permute-start = (bf16[256,1024]{1,0:T(8,128)(2,1)S(1)}, bf16[256,1024]{1,0:T(8,128)(2,1)S(1)}, u32[]{:S(2)}, u32[]{:S(2)}) collective-permute-start(bf16[256,1024]{1,0:T(8,128)(2,1)S(1)} %get-tuple-element.44), channel_id=1, source_target_pairs={{0,128},{8,136},{16,144},{24,152},{32,160},{40,168},{48,176},{56,1... | collective-permute-start | bytes 1572872 | tf_op jit(solution)/shard_map/ppermute | solution.py:10
  27.3 5.7 %collective-permute-start.1 = (bf16[256,1024]{1,0:T(8,128)(2,1)S(1)}, bf16[256,1024]{1,0:T(8,128)(2,1)}, u32[]{:S(2)}, u32[]{:S(2)}) collective-permute-start(bf16[256,1024]{1,0:T(8,128)(2,1)S(1)} %get-tuple-element.45), channel_id=1, source_target_pairs={{0,256},{8,264},{16,272},{24,280},{32,288},{40,296},{48,304},{56,3... | collective-permute-start | bytes 1572872 | tf_op jit(solution)/shard_map/ppermute | solution.py:10
  33.0 5.0 %collective-permute-start.2 = (bf16[256,1024]{1,0:T(8,128)(2,1)S(1)}, bf16[256,1024]{1,0:T(8,128)(2,1)}, u32[]{:S(2)}, u32[]{:S(2)}) collective-permute-start(bf16[256,1024]{1,0:T(8,128)(2,1)S(1)} %get-tuple-element.46), channel_id=1, source_target_pairs={{0,384},{8,392},{16,400},{24,408},{32,416},{40,424},{48,432},{56,4... | collective-permute-start | bytes 1572872 | tf_op jit(solution)/shard_map/ppermute | solution.py:10
  39.0 0.8 slice_reduce_fusion.29
  40.2 1.1 collective-permute-done
  41.2 27.6 %collective-permute-done.1 = bf16[256,1024]{1,0:T(8,128)(2,1)} collective-permute-done((bf16[256,1024]{1,0:T(8,128)(2,1)S(1)}, bf16[256,1024]{1,0:T(8,128)(2,1)}, u32[]{:S(2)}, u32[]{:S(2)}) %collective-permute-start.1) | collective-permute-done | bytes 524320 | tf_op jit(solution)/shard_map/ppermute | solution.py:10
  68.8 11.9 %collective-permute-done.2 = bf16[256,1024]{1,0:T(8,128)(2,1)} collective-permute-done((bf16[256,1024]{1,0:T(8,128)(2,1)S(1)}, bf16[256,1024]{1,0:T(8,128)(2,1)}, u32[]{:S(2)}, u32[]{:S(2)}) %collective-permute-start.2) | collective-permute-done | bytes 524320 | tf_op jit(solution)/shard_map/ppermute | solution.py:10
  80.7 1.5 pad_maximum_fusion
  82.3 2.2 gather_fusion.1
  84.7 31.2 %all-gather.4.cloned.1.call-done = bf16[1536,512]{1,0:T(8,128)(2,1)} async-done(((bf16[24,512]{1,0:T(8,128)(2,1)}), bf16[1536,512]{1,0:T(8,128)(2,1)}) %all-gather.4.cloned.1.call-update) | async-done | bytes 1572880 | tf_op jit(solution)/shard_map/all_gather | solution.py:91
  116.0 1.5 fusion.62
  117.5 2.5 convolution_add_fusion.1
  120.0 78.9 %all-gather.6.cloned.1.call-done = bf16[512,1536]{1,0:T(8,128)(2,1)} async-done(((bf16[8,1536]{1,0:T(8,128)(2,1)}), bf16[512,1536]{1,0:T(8,128)(2,1)}) %all-gather.6.cloned.1.call-update) | async-done | bytes 1572880 | tf_op jit(solution)/shard_map/all_gather | solution.py:92
  198.9 3.2 %convert_reduce_fusion = (f32[512]{0:T(512)S(1)}, bf16[512,1536]{1,0:T(8,128)(2,1)S(1)}) fusion(bf16[512,1536]{1,0:T(8,128)(2,1)} %all-gather.6.cloned.1.call-done, f32[512,512]{1,0:T(8,128)} %convolution_add_fusion.1, bf16[1536,512]{1,0:T(8,128)(2,1)} %all-gather.4.cloned.1.call-done, bf16[512,1024]{1,0:T(8,128)(2,1)S(1)} %broadcast_select_fusion), kind=kOutput, calls=%fused_computation.7 | convolution fusion | flops 1076887040 | bytes 5244928 | tf_op jit(solution)/shard_map/dot_general | solution.py:116
  202.7 59.3 %all-gather.8.cloned.1.call-done = bf16[2,1536,1536]{1,2,0:T(8,128)(2,1)} async-done(((bf16[2,1536,192]{1,2,0:T(8,128)(2,1)}), bf16[2,1536,1536]{1,2,0:T(8,128)(2,1)}) %all-gather.8.cloned.1.call-update) | async-done | bytes 9437200 | tf_op jit(solution)/shard_map/all_gather | solution.py:118
  261.9 5.2 %fusion.7 = f32[512,1536]{1,0:T(8,128)S(1)} fusion(bf16[2,1536,1536]{1,2,0:T(8,128)(2,1)} %all-gather.8.cloned.1.call-done, bf16[512,1536]{1,0:T(8,128)(2,1)S(1)} %get-tuple-element.85, f32[1536]{0:T(1024)S(1)} %copy-done.10, f32[512]{0:T(512)S(1)} %add_rsqrt_fusion.1, f32[512]{0:T(512)S(1)} %broadcast_multiply_fusion.1), kind=kOutput, calls=%fused_computation.13 | convolution fusion | flops 2421424128 | bytes 9447424 | tf_op jit(solution)/shard_map/dot_general | solution.py:51
  267.2 2.7 fusion.53
  269.9 24.0 %fusion.83 = (f32[512]{0:T(512)S(1)}, f32[512,1536]{1,0:T(8,128)S(1)}) fusion(f32[1536]{0:T(1024)S(1)} %copy-done.6, pred[512]{0:T(512)(128)(4,1)S(1)} %get-tuple-element.48, f32[1536]{0:T(1024)S(1)} %copy-done.7, pred[512]{0:T(512)(128)(4,1)S(1)} %get-tuple-element.49, f32[1536]{0:T(1024)S(1)} %get-tuple-element.6, ...), kind=kLoop, calls=%fused_computation.211 | loop fusion | flops 73137664 | bytes 6499840 | tf_op jit(solution)/shard_map/reduce_sum | solution.py:30
  294.6 2.2 multiply_convert_fusion
  (49 shorter events, 5.7 us)
Async XLA Ops:
  6.5 109.4 %all-gather.4.cloned.1.call-start = ((), (), s32[]{:S(2)}) async-start(), calls=%async_computation | async-start | bytes 1597440 | tf_op jit(solution)/shard_map/all_gather | solution.py:91
  7.3 191.6 %all-gather.6.cloned.1.call-start = ((), (), s32[]{:S(2)}) async-start(), calls=%async_computation.1 | async-start | bytes 1597440 | tf_op jit(solution)/shard_map/all_gather | solution.py:92
  8.0 253.9 %all-gather.8.cloned.1.call-start = ((), (), s32[]{:S(2)}) async-start(), calls=%async_computation.2 | async-start | bytes 10616832 | tf_op jit(solution)/shard_map/all_gather | solution.py:118
  8.7 30.2 %copy-start.1 = (f32[31,1536]{1,0:T(8,128)S(1)}, f32[31,1536]{1,0:T(8,128)}, u32[]{:S(2)}) copy-start(f32[31,1536]{1,0:T(8,128)} %param.15) | copy-start | bytes 571396
  22.2 19.0 %collective-permute-start = (bf16[256,1024]{1,0:T(8,128)(2,1)S(1)}, bf16[256,1024]{1,0:T(8,128)(2,1)S(1)}, u32[]{:S(2)}, u32[]{:S(2)}) collective-permute-start(bf16[256,1024]{1,0:T(8,128)(2,1)S(1)} %get-tuple-element.44), channel_id=1, source_target_pairs={{0,128},{8,136},{16,144},{24,152},{32,160},{40,168},{48,176},{56,1... | collective-permute-start | bytes 1572872 | tf_op jit(solution)/shard_map/ppermute | solution.py:10
  27.3 41.5 %collective-permute-start.1 = (bf16[256,1024]{1,0:T(8,128)(2,1)S(1)}, bf16[256,1024]{1,0:T(8,128)(2,1)}, u32[]{:S(2)}, u32[]{:S(2)}) collective-permute-start(bf16[256,1024]{1,0:T(8,128)(2,1)S(1)} %get-tuple-element.45), channel_id=1, source_target_pairs={{0,256},{8,264},{16,272},{24,280},{32,288},{40,296},{48,304},{56,3... | collective-permute-start | bytes 1572872 | tf_op jit(solution)/shard_map/ppermute | solution.py:10
  33.0 47.8 %collective-permute-start.2 = (bf16[256,1024]{1,0:T(8,128)(2,1)S(1)}, bf16[256,1024]{1,0:T(8,128)(2,1)}, u32[]{:S(2)}, u32[]{:S(2)}) collective-permute-start(bf16[256,1024]{1,0:T(8,128)(2,1)S(1)} %get-tuple-element.46), channel_id=1, source_target_pairs={{0,384},{8,392},{16,400},{24,408},{32,416},{40,424},{48,432},{56,4... | collective-permute-start | bytes 1572872 | tf_op jit(solution)/shard_map/ppermute | solution.py:10
  41.2 39.5 %copy-start = (bf16[256,1024]{1,0:T(8,128)(2,1)}, bf16[256,1024]{1,0:T(8,128)(2,1)S(1)}, u32[]{:S(2)}) copy-start(bf16[256,1024]{1,0:T(8,128)(2,1)S(1)} %collective-permute-done) | copy-start | bytes 1572868
  120.0 142.0 %copy-start.10 = (f32[1536]{0:T(1024)S(1)}, f32[1536]{0:T(1024)}, u32[]{:S(2)}) copy-start(f32[1536]{0:T(1024)} %param.16) | copy-start | bytes 18436
  261.9 5.2 %copy-start.9 = (bf16[2,1536,1536]{1,2,0:T(8,128)(2,1)S(1)}, bf16[2,1536,1536]{1,2,0:T(8,128)(2,1)}, u32[]{:S(2)}) copy-start(bf16[2,1536,1536]{1,2,0:T(8,128)(2,1)} %all-gather.8.cloned.1.call-done) | copy-start | bytes 28311556
  267.1 2.8 copy-start.2
  267.1 2.8 copy-start.3
  267.1 2.8 copy-start.4
  267.2 2.8 copy-start.5
  267.2 2.8 copy-start.6
  267.2 2.8 copy-start.7
  293.9 0.7 copy-start.8
Sparse Core Ops, SparseCore 0:
  10.4 105.5 all-gather.3
  119.0 79.7 all-gather.5
  201.0 60.9 all-gather.7
where the time goes:
time: 304 us; the launch traced here: 303 us
  waiting for transfers between devices  212 us (70%)
  other arithmetic  31.5 us (10%)
  between operations  21 us (7%)
  starting transfers between devices  15.8 us (5%)
  matrix products  15 us (5%)
  local copies, waits for them, and re-layouts  7.95 us (3%)
    all_gather x1, waiting for transfers between devices, body(): lax.all_gather(proj_weight, 'dp', axis=0, tiled=True)  78.9 us
    all_gather x1, waiting for transfers between devices, body(): weight_part = lax.all_gather(point_weight, 'fsdp', axis=2, tiled=True)  59.3 us
    ppermute x3, waiting for transfers between devices, passed_along(): return lax.ppermute(value, axis, pairs)  40.6 us
    all_gather x1, waiting for transfers between devices, body(): lax.all_gather(conv_weight, 'dp', axis=0, tiled=True)  31.2 us
    reduce_sum x1, other arithmetic, layer_norm(): centered = values - jnp.mean(values, axis=-1, keepdims=True)  24 us
    ppermute x3, starting transfers between devices, passed_along(): return lax.ppermute(value, axis, pairs)  15.7 us
  transfers between devices with their start and end apart: 6, of which 6 were waited for; matrix products, arithmetic and copies ran while one was open for 7% of the time, Pallas kernels for 0%

commit v1 on v0

--- a/solution.py
+++ b/solution.py
@@ -88,7 +88,9 @@
     slot_counts = jnp.sum(matches * pair_table[:, :, None], axis=1)
     slot_starts = jnp.sum(matches * loader_offsets[:, :, None], axis=1)
     conv_full, proj_full = (
-        lax.all_gather(conv_weight, "dp", axis=0, tiled=True),
+        jnp.concatenate(
+            lax.all_to_all(jnp.stack([conv_weight] * lax.axis_size("dp")), "dp", 0, 0), axis=0
+        ),
         lax.all_gather(proj_weight, "dp", axis=0, tiled=True),
     )
     own_starts = slot_starts[own_index]

time: 304 us -> 237 us (0.78)
  waiting for transfers between devices: 212 us -> 130 us
  starting transfers between devices: 15.8 us -> 31.7 us
    all_gather x1, waiting for transfers between devices: 78.9 us -> 19.6 us  [body(): lax.all_gather(proj_weight, 'dp', axis=0, tiled=True)]
    all_gather x1 -> x0, waiting for transfers between devices: 31.2 us -> none  [body(): lax.all_gather(conv_weight, 'dp', axis=0, tiled=True)]
    all_to_all x0 -> x1, starting transfers between devices: none -> 17.4 us  [body(): lax.all_to_all(jnp.stack([conv_weight] * lax.axis_size('dp')), 'dp', 0, 0)]
    ppermute x3, waiting for transfers between devices: 40.6 us -> 50.2 us  [passed_along(): return lax.ppermute(value, axis, pairs)]
  transfers between devices with their start and end apart: 6 -> 6, of which waited for: 6 -> 4; matrix products, arithmetic and copies ran while one was open for 7% -> 8% of each run, Pallas kernels for 0% -> 0%
where the time goes in v1:
time: 237 us
  waiting for transfers between devices  130 us (55%)
  starting transfers between devices  31.7 us (13%)
  other arithmetic  29.4 us (12%)
  between operations  21.5 us (9%)
  matrix products  15 us (6%)
  local copies, waits for them, and re-layouts  8.92 us (4%)
    all_gather x1, waiting for transfers between devices, body(): weight_part = lax.all_gather(point_weight, 'fsdp', axis=2, tiled=True)  58.9 us
    ppermute x3, waiting for transfers between devices, passed_along(): return lax.ppermute(value, axis, pairs)  50.2 us
    reduce_sum x1, other arithmetic, layer_norm(): centered = values - jnp.mean(values, axis=-1, keepdims=True)  24 us
    all_gather x1, waiting for transfers between devices, body(): lax.all_gather(proj_weight, 'dp', axis=0, tiled=True)  19.6 us
    all_to_all x1, starting transfers between devices, body(): lax.all_to_all(jnp.stack([conv_weight] * lax.axis_size('dp')), 'dp', 0, 0)  17.4 us
    ppermute x3, starting transfers between devices, passed_along(): return lax.ppermute(value, axis, pairs)  14.3 us
    dot_general x1, matrix products, gate_product(): gate_part = jnp.dot(normed, gate_weight, preferred_element_type=jnp.float32)  5.16 us
  transfers between devices with their start and end apart: 6, of which 4 were waited for; matrix products, arithmetic and copies ran while one was open for 8% of the time, Pallas kernels for 0%

profile of v1, /device:TPU:1, one launch (start us, length us, event | category | flops | bytes accessed | tf_op | source)
XLA Modules:
  0.0 236.7 jit_solution(3226328900426013268)
XLA Ops:
  6.5 0.7 all-gather.3.cloned.1.call-update
  7.3 0.7 all-gather.5.cloned.1.call-update
  8.0 2.0 stack.2
  10.0 17.4 %all-to-all-start = ((bf16[64,24,512]{2,1,0:T(8,128)(2,1)}), bf16[64,24,512]{2,1,0:T(8,128)(2,1)}, u32[]{:S(2)}, u32[]{:S(2)}) async-start(bf16[64,24,512]{2,1,0:T(8,128)(2,1)} %stack.2), calls=%async_computation | async-start | bytes 3145728 | tf_op jit(solution)/shard_map/all_to_all | solution.py:92
  27.6 0.6 fusion.84
  36.3 1.6 pad_dynamic-slice_fusion.3
  37.9 3.8 %collective-permute-start = (bf16[256,1024]{1,0:T(8,128)(2,1)S(1)}, bf16[256,1024]{1,0:T(8,128)(2,1)S(1)}, u32[]{:S(2)}, u32[]{:S(2)}) collective-permute-start(bf16[256,1024]{1,0:T(8,128)(2,1)S(1)} %get-tuple-element.44), channel_id=1, source_target_pairs={{0,128},{8,136},{16,144},{24,152},{32,160},{40,168},{48,176},{56,1... | collective-permute-start | bytes 1572872 | tf_op jit(solution)/shard_map/ppermute | solution.py:10
  41.7 5.4 %collective-permute-start.1 = (bf16[256,1024]{1,0:T(8,128)(2,1)S(1)}, bf16[256,1024]{1,0:T(8,128)(2,1)}, u32[]{:S(2)}, u32[]{:S(2)}) collective-permute-start(bf16[256,1024]{1,0:T(8,128)(2,1)S(1)} %get-tuple-element.45), channel_id=1, source_target_pairs={{0,256},{8,264},{16,272},{24,280},{32,288},{40,296},{48,304},{56,3... | collective-permute-start | bytes 1572872 | tf_op jit(solution)/shard_map/ppermute | solution.py:10
  47.1 5.1 %collective-permute-start.2 = (bf16[256,1024]{1,0:T(8,128)(2,1)S(1)}, bf16[256,1024]{1,0:T(8,128)(2,1)}, u32[]{:S(2)}, u32[]{:S(2)}) collective-permute-start(bf16[256,1024]{1,0:T(8,128)(2,1)S(1)} %get-tuple-element.46), channel_id=1, source_target_pairs={{0,384},{8,392},{16,400},{24,408},{32,416},{40,424},{48,432},{56,4... | collective-permute-start | bytes 1572872 | tf_op jit(solution)/shard_map/ppermute | solution.py:10
  52.2 0.6 gather_fusion
  53.2 0.8 slice_reduce_fusion.29
  54.4 27.8 %collective-permute-done = bf16[256,1024]{1,0:T(8,128)(2,1)S(1)} collective-permute-done((bf16[256,1024]{1,0:T(8,128)(2,1)S(1)}, bf16[256,1024]{1,0:T(8,128)(2,1)S(1)}, u32[]{:S(2)}, u32[]{:S(2)}) %collective-permute-start) | collective-permute-done | bytes 524320 | tf_op jit(solution)/shard_map/ppermute | solution.py:10
  82.2 22.4 %collective-permute-done.1 = bf16[256,1024]{1,0:T(8,128)(2,1)} collective-permute-done((bf16[256,1024]{1,0:T(8,128)(2,1)S(1)}, bf16[256,1024]{1,0:T(8,128)(2,1)}, u32[]{:S(2)}, u32[]{:S(2)}) %collective-permute-start.1) | collective-permute-done | bytes 524320 | tf_op jit(solution)/shard_map/ppermute | solution.py:10
  104.6 1.5 pad_maximum_fusion
  106.1 2.2 gather_fusion.1
  108.6 1.5 fusion.62
  110.1 2.5 %convolution_add_fusion.1 = f32[512,512]{1,0:T(8,128)} fusion(f32[512,512]{1,0:T(8,128)S(1)} %fusion.62, bf16[1536,512]{1,0:T(8,128)(2,1)} %bitcast.10, bf16[512,1024]{1,0:T(8,128)(2,1)S(1)} %broadcast_select_fusion), kind=kOutput, calls=%fused_computation.85 | convolution fusion | flops 268697600 | bytes 3145728 | tf_op jit(solution)/shard_map/dot_general | solution.py:20
  112.6 19.6 %all-gather.3.cloned.1.call-done = bf16[512,1536]{1,0:T(8,128)(2,1)} async-done(((bf16[8,1536]{1,0:T(8,128)(2,1)}), bf16[512,1536]{1,0:T(8,128)(2,1)}) %all-gather.3.cloned.1.call-update) | async-done | bytes 1572880 | tf_op jit(solution)/shard_map/all_gather | solution.py:94
  132.2 3.2 %convert_reduce_fusion = (f32[512]{0:T(512)S(1)}, bf16[512,1536]{1,0:T(8,128)(2,1)S(1)}) fusion(bf16[512,1536]{1,0:T(8,128)(2,1)} %all-gather.3.cloned.1.call-done, f32[512,512]{1,0:T(8,128)} %convolution_add_fusion.1, bf16[1536,512]{1,0:T(8,128)(2,1)} %bitcast.10, bf16[512,1024]{1,0:T(8,128)(2,1)S(1)} %broadcast_select_fusion), kind=kOutput, calls=%fused_computation.7 | convolution fusion | flops 1076887040 | bytes 5244928 | tf_op jit(solution)/shard_map/dot_general | solution.py:118
  136.0 58.9 %all-gather.5.cloned.1.call-done = bf16[2,1536,1536]{1,2,0:T(8,128)(2,1)} async-done(((bf16[2,1536,192]{1,2,0:T(8,128)(2,1)}), bf16[2,1536,1536]{1,2,0:T(8,128)(2,1)}) %all-gather.5.cloned.1.call-update) | async-done | bytes 9437200 | tf_op jit(solution)/shard_map/all_gather | solution.py:120
  194.9 5.2 %fusion.7 = f32[512,1536]{1,0:T(8,128)S(1)} fusion(bf16[2,1536,1536]{1,2,0:T(8,128)(2,1)} %all-gather.5.cloned.1.call-done, bf16[512,1536]{1,0:T(8,128)(2,1)S(1)} %get-tuple-element.85, f32[1536]{0:T(1024)S(1)} %copy-done.13, f32[512]{0:T(512)S(1)} %add_rsqrt_fusion.1, f32[512]{0:T(512)S(1)} %broadcast_multiply_fusion.1), kind=kOutput, calls=%fused_computation.13 | convolution fusion | flops 2421424128 | bytes 9447424 | tf_op jit(solution)/shard_map/dot_general | solution.py:51
  200.1 2.7 %fusion.53 = f32[512,1536]{1,0:T(8,128)S(1)} fusion(f32[512,1536]{1,0:T(8,128)S(1)} %fusion.7, bf16[2,1536,1536]{1,2,0:T(8,128)(2,1)S(1)} %copy-done.12, bf16[512,1536]{1,0:T(8,128)(2,1)S(1)} %get-tuple-element.85, f32[1536]{0:T(1024)S(1)} %copy-done.13, f32[512]{0:T(512)S(1)} %add_rsqrt_fusion.1, f32[512]{0:T(512)S(1)} %broadcast_multiply_fusion.1), kind=kOutput, calls=%fused_computation.77 | convolution fusion | flops 2422996992 | bytes 12595200 | tf_op jit(solution)/shard_map/dot_general | solution.py:50
  202.9 24.0 %fusion.83 = (f32[512]{0:T(512)S(1)}, f32[512,1536]{1,0:T(8,128)S(1)}) fusion(f32[1536]{0:T(1024)S(1)} %copy-done.7, pred[512]{0:T(512)(128)(4,1)S(1)} %get-tuple-element.48, f32[1536]{0:T(1024)S(1)} %copy-done.8, pred[512]{0:T(512)(128)(4,1)S(1)} %get-tuple-element.49, f32[1536]{0:T(1024)S(1)} %get-tuple-element.6, ...), kind=kLoop, calls=%fused_computation.211 | loop fusion | flops 73137664 | bytes 6499840 | tf_op jit(solution)/shard_map/reduce_sum | solution.py:30
  227.6 2.2 multiply_convert_fusion
  (55 shorter events, 2.8 us)
Async XLA Ops:
  6.5 20.9 %copy-start.9 = (s32[1,64,4]{1,2,0:T(4,128)S(1)}, s32[1,64,4]{1,2,0:T(4,128)}, u32[]{:S(2)}) copy-start(s32[1,64,4]{1,2,0:T(4,128)} %param.10) | copy-start | bytes 3076
  6.5 20.9 %copy-start.11 = (s32[1,64,4]{1,2,0:T(4,128)S(1)}, s32[1,64,4]{1,2,0:T(4,128)}, u32[]{:S(2)}) copy-start(s32[1,64,4]{1,2,0:T(4,128)} %param.11) | copy-start | bytes 3076
  6.5 26.8 %copy-start = (bf16[1024,512]{1,0:T(8,128)(2,1)S(1)}, bf16[1024,512]{1,0:T(8,128)(2,1)}, u32[]{:S(2)}) copy-start(bf16[1024,512]{1,0:T(8,128)(2,1)} %param.9) | copy-start | bytes 3145732
  6.5 125.6 %all-gather.3.cloned.1.call-start = ((), (), s32[]{:S(2)}) async-start(), calls=%async_computation.1 | async-start | bytes 1597440 | tf_op jit(solution)/shard_map/all_gather | solution.py:94
  7.3 187.6 %all-gather.5.cloned.1.call-start = ((), (), s32[]{:S(2)}) async-start(), calls=%async_computation.2 | async-start | bytes 10616832 | tf_op jit(solution)/shard_map/all_gather | solution.py:120
  10.0 98.6 %all-to-all-start = ((bf16[64,24,512]{2,1,0:T(8,128)(2,1)}), bf16[64,24,512]{2,1,0:T(8,128)(2,1)}, u32[]{:S(2)}, u32[]{:S(2)}) async-start(bf16[64,24,512]{2,1,0:T(8,128)(2,1)} %stack.2), calls=%async_computation | async-start | bytes 3145728 | tf_op jit(solution)/shard_map/all_to_all | solution.py:92
  27.4 25.8 %copy-start.2 = (f32[31,1536]{1,0:T(8,128)S(1)}, f32[31,1536]{1,0:T(8,128)}, u32[]{:S(2)}) copy-start(f32[31,1536]{1,0:T(8,128)} %param.15) | copy-start | bytes 571396
  37.9 44.3 %collective-permute-start = (bf16[256,1024]{1,0:T(8,128)(2,1)S(1)}, bf16[256,1024]{1,0:T(8,128)(2,1)S(1)}, u32[]{:S(2)}, u32[]{:S(2)}) collective-permute-start(bf16[256,1024]{1,0:T(8,128)(2,1)S(1)} %get-tuple-element.44), channel_id=1, source_target_pairs={{0,128},{8,136},{16,144},{24,152},{32,160},{40,168},{48,176},{56,1... | collective-permute-start | bytes 1572872 | tf_op jit(solution)/shard_map/ppermute | solution.py:10
  41.7 62.9 %collective-permute-start.1 = (bf16[256,1024]{1,0:T(8,128)(2,1)S(1)}, bf16[256,1024]{1,0:T(8,128)(2,1)}, u32[]{:S(2)}, u32[]{:S(2)}) collective-permute-start(bf16[256,1024]{1,0:T(8,128)(2,1)S(1)} %get-tuple-element.45), channel_id=1, source_target_pairs={{0,256},{8,264},{16,272},{24,280},{32,288},{40,296},{48,304},{56,3... | collective-permute-start | bytes 1572872 | tf_op jit(solution)/shard_map/ppermute | solution.py:10
  47.1 57.5 %collective-permute-start.2 = (bf16[256,1024]{1,0:T(8,128)(2,1)S(1)}, bf16[256,1024]{1,0:T(8,128)(2,1)}, u32[]{:S(2)}, u32[]{:S(2)}) collective-permute-start(bf16[256,1024]{1,0:T(8,128)(2,1)S(1)} %get-tuple-element.46), channel_id=1, source_target_pairs={{0,384},{8,392},{16,400},{24,408},{32,416},{40,424},{48,432},{56,4... | collective-permute-start | bytes 1572872 | tf_op jit(solution)/shard_map/ppermute | solution.py:10
  82.2 22.4 %copy-start.1 = (bf16[256,1024]{1,0:T(8,128)(2,1)}, bf16[256,1024]{1,0:T(8,128)(2,1)S(1)}, u32[]{:S(2)}) copy-start(bf16[256,1024]{1,0:T(8,128)(2,1)S(1)} %collective-permute-done) | copy-start | bytes 1572868
  112.6 82.3 %copy-start.13 = (f32[1536]{0:T(1024)S(1)}, f32[1536]{0:T(1024)}, u32[]{:S(2)}) copy-start(f32[1536]{0:T(1024)} %param.16) | copy-start | bytes 18436
  194.9 5.2 %copy-start.12 = (bf16[2,1536,1536]{1,2,0:T(8,128)(2,1)S(1)}, bf16[2,1536,1536]{1,2,0:T(8,128)(2,1)}, u32[]{:S(2)}) copy-start(bf16[2,1536,1536]{1,2,0:T(8,128)(2,1)} %all-gather.5.cloned.1.call-done) | copy-start | bytes 28311556
  200.1 2.7 %copy-start.3 = (f32[1536]{0:T(1024)S(1)}, f32[1536]{0:T(1024)}, u32[]{:S(2)}) copy-start(f32[1536]{0:T(1024)} %get-tuple-element.30) | copy-start | bytes 18436
  200.1 2.7 %copy-start.4 = (f32[1536]{0:T(1024)S(1)}, f32[1536]{0:T(1024)}, u32[]{:S(2)}) copy-start(f32[1536]{0:T(1024)} %get-tuple-element.31) | copy-start | bytes 18436
  200.1 2.7 %copy-start.5 = (f32[1536]{0:T(1024)S(1)}, f32[1536]{0:T(1024)}, u32[]{:S(2)}) copy-start(f32[1536]{0:T(1024)} %get-tuple-element.32) | copy-start | bytes 18436
  200.1 2.7 %copy-start.6 = (f32[1536]{0:T(1024)S(1)}, f32[1536]{0:T(1024)}, u32[]{:S(2)}) copy-start(f32[1536]{0:T(1024)} %get-tuple-element.33) | copy-start | bytes 18436
  200.1 2.7 %copy-start.7 = (f32[1536]{0:T(1024)S(1)}, f32[1536]{0:T(1024)}, u32[]{:S(2)}) copy-start(f32[1536]{0:T(1024)} %get-tuple-element.34) | copy-start | bytes 18436
  200.1 2.7 %copy-start.8 = (f32[1536]{0:T(1024)S(1)}, f32[1536]{0:T(1024)}, u32[]{:S(2)}) copy-start(f32[1536]{0:T(1024)} %get-tuple-element.35) | copy-start | bytes 18436
  226.9 0.7 copy-start.10
Sparse Core Ops, SparseCore 0:
  10.4 121.7 all-gather.2
  134.3 60.5 all-gather.4
